TPU v7x, 128 devices: a whole 4x4x4 slice. The times are simulated.
128 devices in a mesh: dp: 8 (over x_lo, y), ctx: 16 (over x_hi, z, core).
Axes of the slice: x: 4 (x_hi: 2, x_lo: 2; x = x_hi * 2 + x_lo), y: 4, z: 4, core: 2. Of those that a mesh axis runs over, the one named last changes fastest.
Arguments:
- enc_feat: bfloat16 [8, 256, 16, 512], P(None, ('dp', 'ctx')), may hold values from -6 to 6
- conv_w: bfloat16 [3, 512, 64], replicated, may hold values from -0.15625 to 0.15625
- w_lat: bfloat16 [64, 3072], replicated, may hold values from -0.75 to 0.75
- q_raw: bfloat16 [8, 4096, 3072], P('dp', 'ctx'), may hold values from -40 to 40
- k_raw: bfloat16 [8, 4096, 3072], P('dp', 'ctx'), may hold values from -40 to 40
- v_in: bfloat16 [8, 4096, 3072], P('dp', 'ctx'), may hold values from -6 to 6
- valid: int32 [8, 16], P('dp', 'ctx'), may hold values from 128 to 256, as said below
- d_out: bfloat16 [8, 4096, 3072], P('dp', 'ctx'), may hold values from -6 to 6
Outputs:
- attn_out: bfloat16 [8, 4096, 3072], P('dp', 'ctx')
- dq: bfloat16 [8, 4096, 3072], P('dp', 'ctx')
- dk: bfloat16 [8, 4096, 3072], P('dp', 'ctx')
- dv: bfloat16 [8, 4096, 3072], P('dp', 'ctx')
- dw_lat: float32 [64, 3072], replicated
Inputs may be any that keep to these rules, and one draw needn't show every extreme that they name: `valid`: the first stretch of every clip is full.
All inputs are finite; a program needn't handle non-finite values.
Results may differ from a plain program's by a relative error of at most 0.03.
Values may be sent and summed in bfloat16 or wider, within the bound.
A program may use at most 128 MiB of HBM per device.

v0:
```python
import math

import jax
import jax.numpy as jnp
from jax import lax
from jax.sharding import PartitionSpec as P

DH = 128
BACK = 4


def from_behind(value, axis, by):
    size = lax.axis_size(axis)
    pairs = [(i, i + by) for i in range(size) if 0 <= i + by < size]
    return lax.ppermute(value, axis, pairs)


def attend(query, keys, vals, grads, allowed):
    count = query.shape[0]
    width = keys.shape[0]
    scale = 1.0 / math.sqrt(DH)
    query_heads = query.reshape(count, -1, DH)
    key_heads = keys.reshape(width, -1, DH)
    value_heads = vals.reshape(width, -1, DH)
    grad_heads = grads.reshape(count, -1, DH)
    scores = (
        jnp.einsum("qhd,khd->hqk", query_heads, key_heads, preferred_element_type=jnp.float32)
        * scale
    )
    scores = jnp.where(allowed[None, None, :], scores, -1e30)
    highest = jnp.max(scores, axis=-1, keepdims=True)
    expo = jnp.exp(scores - highest)
    probs = expo / jnp.sum(expo, axis=-1, keepdims=True)
    probs_low = probs.astype(jnp.bfloat16)
    output = jnp.einsum(
        "hqk,khd->qhd", probs_low, value_heads, preferred_element_type=jnp.float32
    ).astype(jnp.bfloat16)
    grad_probs = jnp.einsum(
        "qhd,khd->hqk", grad_heads, value_heads, preferred_element_type=jnp.float32
    )
    delta = jnp.einsum("qhd,qhd->hq", grad_heads, output, preferred_element_type=jnp.float32)
    grad_scores = (probs * (grad_probs - delta[:, :, None]) * scale).astype(jnp.bfloat16)
    dquery = jnp.einsum(
        "hqk,khd->qhd", grad_scores, key_heads, preferred_element_type=jnp.float32
    ).astype(jnp.bfloat16)
    dkeys = jnp.einsum(
        "hqk,qhd->khd", grad_scores, query_heads, preferred_element_type=jnp.float32
    ).astype(jnp.bfloat16)
    dvals = jnp.einsum(
        "hqk,qhd->khd", probs_low, grad_heads, preferred_element_type=jnp.float32
    ).astype(jnp.bfloat16)
    return (
        output.reshape(count, -1),
        dquery.reshape(count, -1),
        dkeys.reshape(width, -1),
        dvals.reshape(width, -1),
    )


def on_device(enc_feat, conv_w, w_lat, q_raw, k_raw, v_in, valid, d_out):
    frame_count = enc_feat.shape[1]
    prior = from_behind(enc_feat, ("dp", "ctx"), 1)
    extended = jnp.concatenate([prior, enc_feat], axis=1)
    latent = jnp.zeros(enc_feat.shape[:3] + (conv_w.shape[2],), jnp.float32)
    for tap_index in range(3):
        window_feat = extended[:, frame_count - tap_index : 2 * frame_count - tap_index]
        latent = latent + jnp.einsum(
            "cfpe,el->cfpl", window_feat, conv_w[tap_index], preferred_element_type=jnp.float32
        )
    clip_count = enc_feat.shape[0]
    latent_low = latent.astype(jnp.bfloat16).reshape(clip_count, -1, latent.shape[3])
    group_dp = lax.axis_size("dp")
    group_ctx = lax.axis_size("ctx")
    ratio = group_ctx // group_dp
    place_dp = lax.axis_index("dp")
    place_ctx = lax.axis_index("ctx")
    target = place_dp * ratio + place_ctx // group_dp
    select = jnp.arange(group_ctx, dtype=jnp.int32) == target
    buffer = jnp.where(
        select[None, :, None, None], latent_low[:, None], jnp.zeros((), jnp.bfloat16)
    )
    buffer = buffer.reshape((group_dp * group_ctx,) + latent_low.shape[1:])
    received = lax.all_to_all(buffer, ("dp", "ctx"), split_axis=0, concat_axis=0, tiled=True)
    stretch_lat = lax.dynamic_slice_in_dim(received, place_ctx * group_dp, group_dp, 0)
    stretch_lat = stretch_lat.reshape(-1, latent_low.shape[2])
    query = q_raw[0]
    keys = k_raw[0]
    grads = d_out[0]
    count = query.shape[0]
    values = (
        v_in[0].astype(jnp.float32)
        + jnp.dot(stretch_lat, w_lat, preferred_element_type=jnp.float32)
    ).astype(jnp.bfloat16)
    own_block = (keys, values, valid)
    earlier = []
    for distance in range(1, BACK + 1):
        earlier.append(from_behind((keys, values, valid), "ctx", distance))
    ordered = earlier[::-1] + [own_block]
    window_keys = jnp.concatenate([block[0] for block in ordered], axis=0)
    window_values = jnp.concatenate([block[1] for block in ordered], axis=0)
    offsets = jnp.arange(count, dtype=jnp.int32)
    allowed = jnp.concatenate([offsets < block[2][0, 0] for block in ordered], axis=0)
    heads = query.shape[1] // DH
    group_size = math.gcd(heads, 4)
    group_count = heads // group_size

    def split_heads(array):
        return array.reshape(array.shape[0], group_count, group_size * DH).transpose(1, 0, 2)

    def merge_heads(array):
        return array.transpose(1, 0, 2).reshape(array.shape[1], -1)

    def per_group(operands):
        return attend(operands[0], operands[1], operands[2], operands[3], allowed)

    outputs, dqueries, dkeys, dvals = lax.map(
        per_group,
        (
            split_heads(query),
            split_heads(window_keys),
            split_heads(window_values),
            split_heads(grads),
        ),
    )
    attn_out = merge_heads(outputs)
    dq = merge_heads(dqueries)
    dkeys = merge_heads(dkeys)
    dvals = merge_heads(dvals)
    key_total = dkeys[BACK * count :].astype(jnp.float32)
    value_total = dvals[BACK * count :].astype(jnp.float32)
    for distance in range(1, BACK + 1):
        first_row = (BACK - distance) * count
        came_keys, came_values = from_behind(
            (dkeys[first_row : first_row + count], dvals[first_row : first_row + count]),
            "ctx",
            -distance,
        )
        key_total = key_total + came_keys.astype(jnp.float32)
        value_total = value_total + came_values.astype(jnp.float32)
    dk = key_total.astype(jnp.bfloat16)
    dv = value_total.astype(jnp.bfloat16)
    local_grad = lax.dot_general(
        stretch_lat, dv, (((0,), (0,)), ((), ())), preferred_element_type=jnp.float32
    )
    dw_lat = lax.psum(local_grad, ("dp", "ctx"))
    return (attn_out[None], dq[None], dk[None], dv[None], dw_lat)


def solution(mesh):
    placed = (
        P(None, ("dp", "ctx"), None, None),
        P(),
        P(),
        P("dp", "ctx", None),
        P("dp", "ctx", None),
        P("dp", "ctx", None),
        P("dp", "ctx"),
        P("dp", "ctx", None),
    )
    return jax.shard_map(
        on_device,
        mesh=mesh,
        in_specs=placed,
        out_specs=(
            P("dp", "ctx", None),
            P("dp", "ctx", None),
            P("dp", "ctx", None),
            P("dp", "ctx", None),
            P(),
        ),
        check_vma=False,
    )
```

profile of v0, /device:TPU:1, one launch (start us, length us, event | category | flops | bytes accessed | tf_op | source)
XLA Modules:
  0.0 836.9 jit_solution(9588254701283261075)
XLA Ops:
  7.2 5.1 collective-permute-start
  14.0 5.1 collective-permute-start.10
  21.4 7.5 all-to-all-start
  28.9 6.4 collective-permute-start.9
  40.8 4.3 collective-permute-start.7
  45.2 22.0 %all-to-all-done = bf16[128,2,1024]{2,1,0:T(2,128)(2,1)S(1)} async-done(((bf16[128,2,1024]{2,1,0:T(2,128)(2,1)}), bf16[128,2,1024]{2,1,0:T(2,128)(2,1)S(1)}, u32[]{:S(2)}, u32[]{:S(2)}) %all-to-all-start) | async-done | bytes 524320 | tf_op jit(solution)/shard_map/all_to_all | solution.py:83
  69.8 72.1 %collective-permute-done.7 = s32[1,1]{1,0:T(1,128)} collective-permute-done((s32[1,1]{1,0:T(1,128)}, s32[1,1]{1,0:T(1,128)}, u32[]{:S(2)}, u32[]{:S(2)}) %collective-permute-start.7) | collective-permute-done | bytes 36 | tf_op jit(solution)/shard_map/ppermute | solution.py:15
  144.1 9.1 %collective-permute-start.5 = (s32[1,1]{1,0:T(1,128)}, s32[1,1]{1,0:T(1,128)}, u32[]{:S(2)}, u32[]{:S(2)}) collective-permute-start(s32[1,1]{1,0:T(1,128)} %param.16), channel_id=1, source_target_pairs={{0,4},{1,5},{2,6},{3,7},{4,8},{5,9},{6,10},{7,11},{8,12},{9,13},{1... | collective-permute-start | bytes 20 | tf_op jit(solution)/shard_map/ppermute | solution.py:15
  153.6 15.0 %collective-permute-start.8 = (s32[1,1]{1,0:T(1,128)}, s32[1,1]{1,0:T(1,128)}, u32[]{:S(2)}, u32[]{:S(2)}) collective-permute-start(s32[1,1]{1,0:T(1,128)} %param.16), channel_id=1, source_target_pairs={{0,1},{1,2},{2,3},{3,4},{4,5},{5,6},{6,7},{7,8},{8,9},{9,10},{10,1... | collective-permute-start | bytes 20 | tf_op jit(solution)/shard_map/ppermute | solution.py:15
  169.4 7.6 collective-permute-start.1
  183.7 9.0 %collective-permute-start.2 = (bf16[256,3072]{1,0:T(8,128)(2,1)S(1)}, bf16[256,3072]{1,0:T(8,128)(2,1)}, u32[]{:S(2)}, u32[]{:S(2)}) collective-permute-start(bf16[256,3072]{1,0:T(8,128)(2,1)S(1)} %fusion.7), channel_id=1, source_target_pairs={{0,3},{1,4},{2,5},{3,6},{4,7},{5,8},{6,9},{7,10},{8,11},{9,12},{10... | collective-permute-start | bytes 4718600 | tf_op jit(solution)/shard_map/ppermute | solution.py:15
  212.0 31.0 %collective-permute-done.2 = bf16[256,3072]{1,0:T(8,128)(2,1)} collective-permute-done((bf16[256,3072]{1,0:T(8,128)(2,1)S(1)}, bf16[256,3072]{1,0:T(8,128)(2,1)}, u32[]{:S(2)}, u32[]{:S(2)}) %collective-permute-start.2) | collective-permute-done | bytes 1572896 | tf_op jit(solution)/shard_map/ppermute | solution.py:15
  245.7 31.1 %collective-permute-done.3 = bf16[256,3072]{1,0:T(8,128)(2,1)S(1)} collective-permute-done((bf16[256,3072]{1,0:T(8,128)(2,1)S(1)}, bf16[256,3072]{1,0:T(8,128)(2,1)S(1)}, u32[]{:S(2)}, u32[]{:S(2)}) %collective-permute-start.3) | collective-permute-done | bytes 1572896 | tf_op jit(solution)/shard_map/ppermute | solution.py:15
  278.0 16.3 %collective-permute-done.4 = bf16[256,3072]{1,0:T(8,128)(2,1)S(1)} collective-permute-done((bf16[256,3072]{1,0:T(8,128)(2,1)S(1)}, bf16[256,3072]{1,0:T(8,128)(2,1)S(1)}, u32[]{:S(2)}, u32[]{:S(2)}) %collective-permute-start.4) | collective-permute-done | bytes 1572896 | tf_op jit(solution)/shard_map/ppermute | solution.py:15
  296.8 10.3 %copy.34 = bf16[1280,3072]{0,1:T(8,128)(2,1)} copy(bf16[1280,3072]{1,0:T(8,128)(2,1)} %constant_dynamic-update-slice_fusion.4) | data formatting | bytes 15728640 | tf_op jit(solution)/shard_map/concatenate | solution.py:100
  307.1 120.5 %while.16 = (s32[]{:T(128)}, bf16[6,256,512]{1,2,0:T(8,128)(2,1)}, bf16[6,256,512]{1,2,0:T(8,128)(2,1)}, bf16[6,1280,512]{1,2,0:T(8,128)(2,1)}, bf16[6,1280,512]...) while((s32[]{:T(128)}, bf16[6,256,512]{1,2,0:T(8,128)(2,1)}, ...), condition=%wide.region_3.4_spmd, body=%wide.region_0.3_spmd.sunk | while | flops 2029781248 | bytes 69490112 | solution.py:116
  427.6 4.8 fusion.31
  442.9 27.1 %collective-permute-done.20 = bf16[256,3072]{0,1:T(8,128)(2,1)} collective-permute-done((bf16[256,3072]{0,1:T(8,128)(2,1)S(1)}, bf16[256,3072]{0,1:T(8,128)(2,1)}, u32[]{:S(2)}, u32[]{:S(2)}) %collective-permute-start.20) | collective-permute-done | bytes 1572896 | tf_op jit(solution)/shard_map/ppermute | solution.py:15
  471.3 34.5 %collective-permute-done.19 = bf16[256,3072]{0,1:T(8,128)(2,1)} collective-permute-done((bf16[256,3072]{0,1:T(8,128)(2,1)S(1)}, bf16[256,3072]{0,1:T(8,128)(2,1)}, u32[]{:S(2)}, u32[]{:S(2)}) %collective-permute-start.19) | collective-permute-done | bytes 1572896 | tf_op jit(solution)/shard_map/ppermute | solution.py:15
  507.1 85.0 %collective-permute-done.18 = bf16[256,3072]{0,1:T(8,128)(2,1)} collective-permute-done((bf16[256,3072]{0,1:T(8,128)(2,1)S(1)}, bf16[256,3072]{0,1:T(8,128)(2,1)}, u32[]{:S(2)}, u32[]{:S(2)}) %collective-permute-start.18) | collective-permute-done | bytes 1572896 | tf_op jit(solution)/shard_map/ppermute | solution.py:15
  599.4 4.5 collective-permute-done.17
  610.5 61.8 %collective-permute-done.14 = bf16[256,3072]{0,1:T(8,128)(2,1)} collective-permute-done((bf16[256,3072]{0,1:T(8,128)(2,1)}, bf16[256,3072]{0,1:T(8,128)(2,1)}, u32[]{:S(2)}, u32[]{:S(2)}) %collective-permute-start.14) | collective-permute-done | bytes 1572896 | tf_op jit(solution)/shard_map/ppermute | solution.py:15
  675.2 4.3 fusion.16
  682.9 145.1 %all-reduce.2.cloned.1.call-done = f32[64,3072]{1,0:T(8,128)} async-done(((f32[64,3072]{1,0:T(8,128)}), f32[64,3072]{1,0:T(8,128)}) %all-reduce.2.cloned.1.call-update) | async-done | bytes 786448 | tf_op jit(solution)/shard_map/psum | solution.py:145
  (202 shorter events, 202.3 us)
Async XLA Ops:
  7.2 12.2 %collective-permute-start = (bf16[8,2,16,512]{3,2,1,0:T(8,128)(2,1)}, bf16[8,2,16,512]{3,2,1,0:T(8,128)(2,1)S(1)}, u32[]{:S(2)}, u32[]{:S(2)}) collective-permute-start(bf16[8,2,16,512]{3,2,1,0:T(8,128)(2,1)} %param.10), channel_id=1, source_target_pairs={{0,1},{1,2},{2,3},{3,4},{4,5},{5,6},{6,7},{7,8},{8,9},{9,10},{10,1... | collective-permute-start | bytes 786440 | tf_op jit(solution)/shard_map/ppermute | solution.py:15
  14.0 169.8 %collective-permute-start.10 = (bf16[256,3072]{0,1:T(8,128)(2,1)S(1)}, bf16[256,3072]{0,1:T(8,128)(2,1)}, u32[]{:S(2)}, u32[]{:S(2)}) collective-permute-start(bf16[256,3072]{0,1:T(8,128)(2,1)S(1)} %bitcast.180), channel_id=1, source_target_pairs={{0,3},{1,4},{2,5},{3,6},{4,7},{5,8},{6,9},{7,10},{8,11},{9,12},{10... | collective-permute-start | bytes 4718600 | tf_op jit(solution)/shard_map/ppermute | solution.py:15
  21.4 45.8 %all-to-all-start = ((bf16[128,2,1024]{2,1,0:T(2,128)(2,1)}), bf16[128,2,1024]{2,1,0:T(2,128)(2,1)S(1)}, u32[]{:S(2)}, u32[]{:S(2)}) async-start(bf16[128,2,1024]{2,1,0:T(2,128)(2,1)} %reshape.88), calls=%async_computation | async-start | bytes 1048576 | tf_op jit(solution)/shard_map/all_to_all | solution.py:83
  28.9 799.1 %all-reduce.2.cloned.1.call-start = ((), (), s32[]{:S(2)}) async-start(), calls=%async_computation.1 | async-start | bytes 1572864 | tf_op jit(solution)/shard_map/psum | solution.py:145
  28.9 166.5 %collective-permute-start.9 = (bf16[256,3072]{0,1:T(8,128)(2,1)S(1)}, bf16[256,3072]{0,1:T(8,128)(2,1)}, u32[]{:S(2)}, u32[]{:S(2)}) collective-permute-start(bf16[256,3072]{0,1:T(8,128)(2,1)S(1)} %bitcast.181), channel_id=1, source_target_pairs={{0,4},{1,5},{2,6},{3,7},{4,8},{5,9},{6,10},{7,11},{8,12},{9,13},{1... | collective-permute-start | bytes 4718600 | tf_op jit(solution)/shard_map/ppermute | solution.py:15
  35.3 164.5 %collective-permute-start.11 = (bf16[256,3072]{0,1:T(8,128)(2,1)S(1)}, bf16[256,3072]{0,1:T(8,128)(2,1)}, u32[]{:S(2)}, u32[]{:S(2)}) collective-permute-start(bf16[256,3072]{0,1:T(8,128)(2,1)S(1)} %bitcast.182), channel_id=1, source_target_pairs={{0,2},{1,3},{2,4},{3,5},{4,6},{5,7},{6,8},{7,9},{8,10},{9,11},{10,... | collective-permute-start | bytes 4718600 | tf_op jit(solution)/shard_map/ppermute | solution.py:15
  38.9 164.5 %collective-permute-start.12 = (bf16[256,3072]{0,1:T(8,128)(2,1)S(1)}, bf16[256,3072]{0,1:T(8,128)(2,1)}, u32[]{:S(2)}, u32[]{:S(2)}) collective-permute-start(bf16[256,3072]{0,1:T(8,128)(2,1)S(1)} %bitcast.183), channel_id=1, source_target_pairs={{0,1},{1,2},{2,3},{3,4},{4,5},{5,6},{6,7},{7,8},{8,9},{9,10},{10,1... | collective-permute-start | bytes 4718600 | tf_op jit(solution)/shard_map/ppermute | solution.py:15
  40.8 101.1 %collective-permute-start.7 = (s32[1,1]{1,0:T(1,128)}, s32[1,1]{1,0:T(1,128)}, u32[]{:S(2)}, u32[]{:S(2)}) collective-permute-start(s32[1,1]{1,0:T(1,128)} %param.16), channel_id=1, source_target_pairs={{0,2},{1,3},{2,4},{3,5},{4,6},{5,7},{6,8},{7,9},{8,10},{9,11},{10,... | collective-permute-start | bytes 20 | tf_op jit(solution)/shard_map/ppermute | solution.py:15
  142.0 2.1 collective-permute-start.6
  144.1 9.4 %collective-permute-start.5 = (s32[1,1]{1,0:T(1,128)}, s32[1,1]{1,0:T(1,128)}, u32[]{:S(2)}, u32[]{:S(2)}) collective-permute-start(s32[1,1]{1,0:T(1,128)} %param.16), channel_id=1, source_target_pairs={{0,4},{1,5},{2,6},{3,7},{4,8},{5,9},{6,10},{7,11},{8,12},{9,13},{1... | collective-permute-start | bytes 20 | tf_op jit(solution)/shard_map/ppermute | solution.py:15
  153.6 15.9 %collective-permute-start.8 = (s32[1,1]{1,0:T(1,128)}, s32[1,1]{1,0:T(1,128)}, u32[]{:S(2)}, u32[]{:S(2)}) collective-permute-start(s32[1,1]{1,0:T(1,128)} %param.16), channel_id=1, source_target_pairs={{0,1},{1,2},{2,3},{3,4},{4,5},{5,6},{6,7},{7,8},{8,9},{9,10},{10,1... | collective-permute-start | bytes 20 | tf_op jit(solution)/shard_map/ppermute | solution.py:15
  169.4 39.9 %collective-permute-start.1 = (bf16[256,3072]{1,0:T(8,128)(2,1)S(1)}, bf16[256,3072]{1,0:T(8,128)(2,1)}, u32[]{:S(2)}, u32[]{:S(2)}) collective-permute-start(bf16[256,3072]{1,0:T(8,128)(2,1)S(1)} %fusion.7), channel_id=1, source_target_pairs={{0,4},{1,5},{2,6},{3,7},{4,8},{5,9},{6,10},{7,11},{8,12},{9,13},{1... | collective-permute-start | bytes 4718600 | tf_op jit(solution)/shard_map/ppermute | solution.py:15
  183.7 59.3 %collective-permute-start.2 = (bf16[256,3072]{1,0:T(8,128)(2,1)S(1)}, bf16[256,3072]{1,0:T(8,128)(2,1)}, u32[]{:S(2)}, u32[]{:S(2)}) collective-permute-start(bf16[256,3072]{1,0:T(8,128)(2,1)S(1)} %fusion.7), channel_id=1, source_target_pairs={{0,3},{1,4},{2,5},{3,6},{4,7},{5,8},{6,9},{7,10},{8,11},{9,12},{10... | collective-permute-start | bytes 4718600 | tf_op jit(solution)/shard_map/ppermute | solution.py:15
  195.4 81.4 %collective-permute-start.3 = (bf16[256,3072]{1,0:T(8,128)(2,1)S(1)}, bf16[256,3072]{1,0:T(8,128)(2,1)S(1)}, u32[]{:S(2)}, u32[]{:S(2)}) collective-permute-start(bf16[256,3072]{1,0:T(8,128)(2,1)S(1)} %fusion.7), channel_id=1, source_target_pairs={{0,2},{1,3},{2,4},{3,5},{4,6},{5,7},{6,8},{7,9},{8,10},{9,11},{10,... | collective-permute-start | bytes 4718600 | tf_op jit(solution)/shard_map/ppermute | solution.py:15
  199.9 94.4 %collective-permute-start.4 = (bf16[256,3072]{1,0:T(8,128)(2,1)S(1)}, bf16[256,3072]{1,0:T(8,128)(2,1)S(1)}, u32[]{:S(2)}, u32[]{:S(2)}) collective-permute-start(bf16[256,3072]{1,0:T(8,128)(2,1)S(1)} %fusion.7), channel_id=1, source_target_pairs={{0,1},{1,2},{2,3},{3,4},{4,5},{5,6},{6,7},{7,8},{8,9},{9,10},{10,1... | collective-permute-start | bytes 4718600 | tf_op jit(solution)/shard_map/ppermute | solution.py:15
  432.4 37.6 %collective-permute-start.20 = (bf16[256,3072]{0,1:T(8,128)(2,1)S(1)}, bf16[256,3072]{0,1:T(8,128)(2,1)}, u32[]{:S(2)}, u32[]{:S(2)}) collective-permute-start(bf16[256,3072]{0,1:T(8,128)(2,1)S(1)} %bitcast.191), channel_id=1, source_target_pairs={{4,0},{5,1},{6,2},{7,3},{8,4},{9,5},{10,6},{11,7},{12,8},{13,9},{1... | collective-permute-start | bytes 4718600 | tf_op jit(solution)/shard_map/ppermute | solution.py:15
  433.8 72.0 %collective-permute-start.19 = (bf16[256,3072]{0,1:T(8,128)(2,1)S(1)}, bf16[256,3072]{0,1:T(8,128)(2,1)}, u32[]{:S(2)}, u32[]{:S(2)}) collective-permute-start(bf16[256,3072]{0,1:T(8,128)(2,1)S(1)} %bitcast.190), channel_id=1, source_target_pairs={{3,0},{4,1},{5,2},{6,3},{7,4},{8,5},{9,6},{10,7},{11,8},{12,9},{13... | collective-permute-start | bytes 4718600 | tf_op jit(solution)/shard_map/ppermute | solution.py:15
  435.1 157.1 %collective-permute-start.18 = (bf16[256,3072]{0,1:T(8,128)(2,1)S(1)}, bf16[256,3072]{0,1:T(8,128)(2,1)}, u32[]{:S(2)}, u32[]{:S(2)}) collective-permute-start(bf16[256,3072]{0,1:T(8,128)(2,1)S(1)} %bitcast.189), channel_id=1, source_target_pairs={{2,0},{3,1},{4,2},{5,3},{6,4},{7,5},{8,6},{9,7},{10,8},{11,9},{12,... | collective-permute-start | bytes 4718600 | tf_op jit(solution)/shard_map/ppermute | solution.py:15
  436.4 167.6 %collective-permute-start.17 = (bf16[256,3072]{0,1:T(8,128)(2,1)}, bf16[256,3072]{0,1:T(8,128)(2,1)S(1)}, u32[]{:S(2)}, u32[]{:S(2)}) collective-permute-start(bf16[256,3072]{0,1:T(8,128)(2,1)} %bitcast.60), channel_id=1, source_target_pairs={{1,0},{2,1},{3,2},{4,3},{5,4},{6,5},{7,6},{8,7},{9,8},{10,9},{11,1... | collective-permute-start | bytes 4718600 | tf_op jit(solution)/shard_map/ppermute | solution.py:15
  441.6 168.9 %collective-permute-start.16 = (bf16[256,3072]{0,1:T(8,128)(2,1)}, bf16[256,3072]{0,1:T(8,128)(2,1)}, u32[]{:S(2)}, u32[]{:S(2)}) collective-permute-start(bf16[256,3072]{0,1:T(8,128)(2,1)} %bitcast.56), channel_id=1, source_target_pairs={{4,0},{5,1},{6,2},{7,3},{8,4},{9,5},{10,6},{11,7},{12,8},{13,9},{1... | collective-permute-start | bytes 4718600 | tf_op jit(solution)/shard_map/ppermute | solution.py:15
  470.0 140.5 %collective-permute-start.15 = (bf16[256,3072]{0,1:T(8,128)(2,1)}, bf16[256,3072]{0,1:T(8,128)(2,1)}, u32[]{:S(2)}, u32[]{:S(2)}) collective-permute-start(bf16[256,3072]{0,1:T(8,128)(2,1)} %bitcast.55), channel_id=1, source_target_pairs={{3,0},{4,1},{5,2},{6,3},{7,4},{8,5},{9,6},{10,7},{11,8},{12,9},{13... | collective-permute-start | bytes 4718600 | tf_op jit(solution)/shard_map/ppermute | solution.py:15
  505.8 166.4 %collective-permute-start.14 = (bf16[256,3072]{0,1:T(8,128)(2,1)}, bf16[256,3072]{0,1:T(8,128)(2,1)}, u32[]{:S(2)}, u32[]{:S(2)}) collective-permute-start(bf16[256,3072]{0,1:T(8,128)(2,1)} %bitcast.54), channel_id=1, source_target_pairs={{2,0},{3,1},{4,2},{5,3},{6,4},{7,5},{8,6},{9,7},{10,8},{11,9},{12,... | collective-permute-start | bytes 4718600 | tf_op jit(solution)/shard_map/ppermute | solution.py:15
  592.1 83.0 %collective-permute-start.13 = (bf16[256,3072]{0,1:T(8,128)(2,1)}, bf16[256,3072]{0,1:T(8,128)(2,1)}, u32[]{:S(2)}, u32[]{:S(2)}) collective-permute-start(bf16[256,3072]{0,1:T(8,128)(2,1)} %bitcast.53), channel_id=1, source_target_pairs={{1,0},{2,1},{3,2},{4,3},{5,4},{6,5},{7,6},{8,7},{9,8},{10,9},{11,1... | collective-permute-start | bytes 4718600 | tf_op jit(solution)/shard_map/ppermute | solution.py:15
  681.2 148.9 %copy-start.1 = (bf16[64,3072]{1,0:T(8,128)(2,1)S(1)}, bf16[64,3072]{1,0:T(8,128)(2,1)}, u32[]{:S(2)}) copy-start(bf16[64,3072]{1,0:T(8,128)(2,1)} %param.12) | copy-start | bytes 1179652
  (21 other events, 227.7 us)
Sparse Core Ops, SparseCore 0:
  610.6 217.3 all-reduce.1
where the time goes:
time: 839 us; the launch traced here: 837 us
  waiting for transfers between devices  539 us (64%)
  local copies, waits for them, and re-layouts  99 us (12%)
  starting transfers between devices  91.7 us (11%)
  matrix products  57.4 us (7%)
  other arithmetic  34 us (4%)
  between operations  15.1 us (2%)
    ppermute x21, waiting for transfers between devices, from_behind(): return lax.ppermute(value, axis, pairs)  372 us
    psum x1, waiting for transfers between devices, on_device(): dw_lat = lax.psum(local_grad, ('dp', 'ctx'))  145 us
    ppermute x21, starting transfers between devices, from_behind(): return lax.ppermute(value, axis, pairs)  84.2 us
    unnamed x42, local copies, waits for them, and re-layouts  35.6 us
    dynamic_slice x24, local copies, waits for them, and re-layouts, on_device(): lax.map(per_group, (split_heads(query), split_heads(window_keys), split_h...  28.5 us
    sub x6, matrix products, attend(): expo = jnp.exp(scores - highest)  25 us
    convert_element_type x6, other arithmetic, attend(): probs_low = probs.astype(jnp.bfloat16)  23.1 us
    all_to_all x1, waiting for transfers between devices, on_device(): lax.all_to_all(buffer, ('dp', 'ctx'), split_axis=0, concat_axis=0, tiled=...  22 us
  transfers between devices with their start and end apart: 23, of which 16 were waited for; matrix products, arithmetic and copies ran while one was open for 6% of the time, Pallas kernels for 0%

commit v1 on v0

v1 whole, which is shorter than its diff:
```python
import math

import jax
import jax.numpy as jnp
from jax import lax
from jax.experimental import pallas as pl
from jax.experimental.pallas import tpu as pltpu
from jax.sharding import PartitionSpec as P

MESH = pl.DeviceIdType.MESH
DH = 128
ROWS = 256
GROUP = 8
HEADS = 3
BACK = 4
HALO = BACK * ROWS
OWN = GROUP * ROWS
SPAN = (BACK + 1) * ROWS
SCALE = 1.0 / math.sqrt(DH)
EXP2 = SCALE * math.log2(math.e)
MASKED = -1e30
F32 = jnp.float32
BF16 = jnp.bfloat16


def last_last(a, b):
    return lax.dot_general(a, b, (((1,), (1,)), ((), ())), preferred_element_type=F32)


def first_first(a, b):
    return lax.dot_general(a, b, (((0,), (0,)), ((), ())), preferred_element_type=F32)


def dot(a, b):
    return jnp.dot(a, b, preferred_element_type=F32)


def kernel(
    valid_ref, feat_ref, wcat_ref, wlat_ref, q_ref, k_ref, v_ref, do_ref,
    out_ref, dq_ref, dk_ref, dv_ref, dw_ref,
    qb, dob, kb, vb, acc_k, acc_v, stg, part_out, part_in, bias, vbuf, w2, lbuf,
    pk_out, pk_in, dwp, rsb, agb, plb,
    in_s, in_r, fin_s, fin_r, halo_s, halo_r, part_s, part_r, val_s, val_r,
    lat_s, lat_r, enc_s, enc_r, rs_s, rs_r, ag_s, ag_r, pl_s, pl_r, loc,
):
    dp = lax.axis_index("dp")
    ctx = lax.axis_index("ctx")
    xhi = ctx // GROUP
    g = ctx % GROUP
    first = xhi == 0
    partner = (dp, ctx + GROUP - 2 * GROUP * xhi)
    slab_stretch = dp * 2 + xhi
    next_stretch = (slab_stretch + 1) % 16
    self_main = ctx == slab_stretch
    self_carry = ctx == next_stretch
    last_slab = g == GROUP - 1

    def remote(src, dst, ss, rs, dev):
        return pltpu.make_async_remote_copy(
            src_ref=src, dst_ref=dst, send_sem=ss, recv_sem=rs, device_id=dev,
            device_id_type=MESH)

    def local(src, dst, sem):
        return pltpu.make_async_copy(src, dst, sem)

    def await_bytes(ref, sem):
        pltpu.make_async_copy(ref, ref, sem).wait()

    def peer(n):
        return (g + n) % GROUP

    def group_dev(p):
        return (dp, xhi * GROUP + p)

    def loop(lo, hi, body):
        lax.fori_loop(lo, hi, lambda i, c: (body(i), c)[1], 0)

    barrier = pltpu.get_barrier_semaphore()

    def signal(dev):
        pl.semaphore_signal(barrier, inc=1, device_id=dev, device_id_type=MESH)

    loop(1, GROUP, lambda n: signal(group_dev(peer(n))))

    def plane_dev(n):
        m = (dp * 2 + xhi + n) % 16
        return (m // 2, (m % 2) * GROUP + g)

    loop(1, 16, lambda n: signal(plane_dev(n)))
    src_dp = ctx // 2
    src_ctx = (ctx % 2) * GROUP

    def signal_source(i):
        @pl.when(jnp.logical_or(src_dp != dp, src_ctx + i != ctx))
        def _():
            signal((src_dp, src_ctx + i))

    loop(0, GROUP, signal_source)
    prev = (ctx + 15) % 16
    prev_dp = prev // 2
    prev_ctx = (prev % 2) * GROUP + GROUP - 1

    @pl.when(jnp.logical_or(prev_dp != dp, prev_ctx != ctx))
    def _():
        signal((prev_dp, prev_ctx))

    one = jnp.int32(1)
    zero = jnp.int32(0)
    expected = (
        (GROUP - 1) + 15 + 8 - jnp.where(self_main, one, zero)
        + jnp.where(last_slab, 8 - jnp.where(self_carry, one, zero), zero)
    )

    local(wlat_ref.at[:, pl.ds(pl.multiple_of(g * HEADS * DH, DH), HEADS * DH)],
          w2.at[pl.ds(64, 64)], loc.at[0]).start()
    a4 = dot(feat_ref[...], wcat_ref[:, 0:128]).reshape(8, 2, 16, 128)
    b4 = dot(feat_ref[...], wcat_ref[:, 128:256]).reshape(8, 2, 16, 128)
    mix = a4[:, 1] + b4[:, 0]
    low = lax.broadcasted_iota(jnp.int32, (8, 16, 128), 2) < 64
    pk_out[:, 0:16, :] = jnp.where(low, a4[:, 0], mix)
    pk_out[:, 16:32, :] = jnp.where(low, mix, b4[:, 1])

    pl.semaphore_wait(barrier, expected)

    def main_copy(c):
        return remote(pk_out.at[c], pk_in.at[1 + g], enc_s.at[0, c], enc_r.at[0],
                      (c, slab_stretch))

    def carry_copy(c):
        return remote(pk_out.at[c], pk_in.at[0], enc_s.at[1, c], enc_r.at[0],
                      (c, next_stretch))

    def is_self(c, own):
        return jnp.logical_and(own, c == dp)

    def send_main(c):
        @pl.when(is_self(c, self_main))
        def _():
            local(pk_out.at[c], pk_in.at[1 + g], enc_r.at[0]).start()

        @pl.when(jnp.logical_not(is_self(c, self_main)))
        def _():
            main_copy(c).start()

    def send_carry(c):
        @pl.when(is_self(c, self_carry))
        def _():
            local(pk_out.at[c], pk_in.at[0], enc_r.at[0]).start()

        @pl.when(jnp.logical_not(is_self(c, self_carry)))
        def _():
            carry_copy(c).start()

    loop(0, 8, send_main)

    @pl.when(last_slab)
    def _():
        loop(0, 8, send_carry)

    local(valid_ref, vbuf.at[BACK + g], val_r.at[0]).start()
    loop(1, GROUP, lambda n: remote(
        valid_ref, vbuf.at[BACK + g], val_s.at[0], val_r.at[0],
        group_dev(peer(n))).start())

    arrays = ((k_ref, kb, HALO), (q_ref, qb, 0), (do_ref, dob, 0), (v_ref, vb, HALO))

    def send_head(h):
        for a, (src, buf, off) in enumerate(arrays):
            dst = buf.at[h, pl.ds(pl.multiple_of(off + g * ROWS, ROWS), ROWS)]

            def cols(p):
                return src.at[:, pl.ds(pl.multiple_of((HEADS * p + h) * DH, DH), DH)]

            local(cols(g), dst, in_r.at[h, a]).start()
            loop(1, GROUP, lambda n: remote(
                cols(peer(n)), dst, in_s.at[h, a], in_r.at[h, a],
                group_dev(peer(n))).start())

    send_head(0)

    w2[0:64, :] = jnp.zeros((64, HEADS * DH), BF16)
    w2[128:192, :] = jnp.zeros((64, HEADS * DH), BF16)

    @pl.when(first)
    def _():
        kb[:, 0:HALO, :] = jnp.zeros((HEADS, HALO, DH), BF16)
        vb[:, 0:HALO, :] = jnp.zeros((HEADS, HALO, DH), BF16)
        vbuf[0:BACK] = jnp.zeros((BACK, 8, 128), jnp.int32)

    await_bytes(pk_in, enc_r.at[0])
    before = jnp.concatenate(
        [jnp.where(ctx == 0, jnp.zeros((1, 32, 128), F32), pk_in[0:1]), pk_in[1:8]], axis=0)
    x = (pk_in[1:9] + pltpu.roll(before, 64, 2)).reshape(ROWS, 128)
    lat_low = lax.broadcasted_iota(jnp.int32, (128, 128), 1) < 64
    lbuf[g] = jnp.where(lat_low, x[0:128], pltpu.roll(x[128:256], 64, 1)).astype(BF16)
    loop(1, GROUP, lambda n: remote(
        lbuf.at[g], lbuf.at[g], lat_s.at[0], lat_r.at[0], group_dev(peer(n))).start())

    send_head(1)
    send_head(2)

    await_bytes(vbuf.at[BACK:], val_r.at[0])
    halo_valid = remote(vbuf.at[pl.ds(GROUP, BACK)], vbuf.at[pl.ds(0, BACK)],
                        val_s.at[1], val_r.at[1], partner)

    @pl.when(first)
    def _():
        halo_valid.start()

    @pl.when(jnp.logical_not(first))
    def _():
        await_bytes(vbuf.at[0:BACK], val_r.at[1])

    def make_bias(s):
        rows = lax.broadcasted_iota(jnp.int32, (ROWS, 128), 0)
        ok = rows < vbuf[s, 0:1, :]
        col = jnp.where(ok, jnp.zeros((ROWS, 128), F32), jnp.full((ROWS, 128), MASKED, F32))
        at = pl.ds(pl.multiple_of(s * ROWS, ROWS), ROWS)
        bias[at, 0:128] = col
        bias[at, 128:256] = col

    loop(0, BACK + GROUP, make_bias)
    local(wlat_ref.at[:, pl.ds(0, HEADS * DH)], w2.at[pl.ds(64, 64)], loc.at[0]).wait()
    await_bytes(lbuf.at[0:GROUP - 1], lat_r.at[0])

    def halo_copy(h, a):
        buf = (kb, vb)[a]
        return remote(buf.at[h, pl.ds(OWN, HALO)], buf.at[h, pl.ds(0, HALO)],
                      halo_s.at[h, a], halo_r.at[h, a], partner)

    def part_copy(h):
        return remote(part_out.at[h], part_in.at[h], part_s.at[h], part_r.at[h], partner)

    def send_result(h, a, s):
        ref = (out_ref, dq_ref, dk_ref, dv_ref)[a]
        src = stg.at[a, h, pl.ds(pl.multiple_of(s * ROWS, ROWS), ROWS)]
        dst = ref.at[:, pl.ds(pl.multiple_of((HEADS * g + h) * DH, DH), DH)]

        @pl.when(s == g)
        def _():
            local(src, dst, fin_r.at[a]).start()

        @pl.when(s != g)
        def _():
            remote(src, dst, fin_s.at[h, a], fin_r.at[a], group_dev(s)).start()

    def stretch(h, i):
        rows = pl.ds(pl.multiple_of(i * ROWS, ROWS), ROWS)
        span = pl.ds(pl.multiple_of(i * ROWS, ROWS), SPAN)
        q = qb[h, rows]
        do = dob[h, rows]
        keys = kb[h, span]
        vals = vb[h, span]
        s = last_last(keys, q) + bias[span, :]
        m = jnp.max(s, axis=0, keepdims=True)
        e = jnp.exp2((s - m) * EXP2)
        p = e * (1.0 / jnp.sum(e, axis=0, keepdims=True))
        p_low = p.astype(BF16)
        out_t = first_first(vals, p_low)
        out = out_t.T.astype(BF16)
        stg[0, h, rows] = out
        delta = jnp.sum(do.astype(F32).T * out_t.astype(BF16).astype(F32), axis=0, keepdims=True)
        grad = last_last(vals, do)
        ds = (p * (grad - delta)).astype(BF16)
        stg[1, h, rows] = (first_first(keys, ds) * SCALE).T.astype(BF16)
        acc_k[h, span] += dot(ds, q)
        acc_v[h, span] += dot(p_low, do)
        send_result(h, 0, i)
        send_result(h, 1, i)

    def finish(h, s, with_part):
        rows = pl.ds(pl.multiple_of(HALO + s * ROWS, ROWS), ROWS)
        dk = acc_k[h, rows] * SCALE
        dv = acc_v[h, rows]
        if with_part:
            at = pl.ds(pl.multiple_of((s - BACK) * ROWS, ROWS), ROWS)
            dk = dk + part_in[h, 0, at].astype(F32)
            dv = dv + part_in[h, 1, at].astype(F32)
        own = pl.ds(pl.multiple_of(s * ROWS, ROWS), ROWS)
        stg[2, h, own] = dk.astype(BF16)
        stg[3, h, own] = dv.astype(BF16)
        send_result(h, 2, s)
        send_result(h, 3, s)

    def owner_of(h):
        return h % 2

    def rs_copy(h, j):
        return remote(
            dwp.at[h, pl.ds(pl.multiple_of(8 * j, 8), 8)], rsb.at[h, dp * 2 + xhi],
            rs_s.at[h, j], rs_r.at[h], (j, owner_of(h) * GROUP + g))

    def rs_self(h, j):
        return jnp.logical_and(j == dp, xhi == owner_of(h))

    def late(h):
        @pl.when(first)
        def _():
            await_bytes(part_in.at[h], part_r.at[h])
            loop(BACK, GROUP, lambda s: finish(h, s, True))

        def add(s, carry):
            top, bottom = carry
            at = pl.multiple_of(s * ROWS, ROWS)
            lat = lbuf[s]
            top = top + first_first(lat, stg[3, h, pl.ds(at, 128)])
            bottom = bottom + first_first(lat, stg[3, h, pl.ds(at + 128, 128)])
            return top, bottom

        zeros = jnp.zeros((128, 128), F32)
        top, bottom = lax.fori_loop(0, GROUP, add, (zeros, zeros))
        dwp[h] = top[0:64] + bottom[64:128]

        def send(j):
            @pl.when(rs_self(h, j))
            def _():
                local(dwp.at[h, pl.ds(pl.multiple_of(8 * j, 8), 8)],
                      rsb.at[h, dp * 2 + xhi], rs_r.at[h]).start()

            @pl.when(jnp.logical_not(rs_self(h, j)))
            def _():
                rs_copy(h, j).start()

        loop(0, 8, send)

    def head(h):
        for a, (_, buf, off) in enumerate(arrays):
            await_bytes(buf.at[h, pl.ds(off, OWN)], in_r.at[h, a])

        def add_latents(s):
            lat = lbuf[s]
            at = pl.multiple_of(HALO + s * ROWS, ROWS)
            cols = pl.ds(pl.multiple_of(h * DH, DH), DH)
            upper = pl.ds(at, 128)
            lower = pl.ds(at + 128, 128)
            vb[h, upper] = (vb[h, upper].astype(F32) + dot(lat, w2[64:192, cols])).astype(BF16)
            vb[h, lower] = (vb[h, lower].astype(F32) + dot(lat, w2[0:128, cols])).astype(BF16)

        @pl.when(first)
        def _():
            halo_copy(h, 0).start()

        loop(0, GROUP, add_latents)

        @pl.when(first)
        def _():
            halo_copy(h, 1).start()

        acc_k[h] = jnp.zeros((HALO + OWN, DH), F32)
        acc_v[h] = jnp.zeros((HALO + OWN, DH), F32)

        loop(BACK, GROUP, lambda i: stretch(h, i))

        @pl.when(jnp.logical_not(first))
        def _():
            await_bytes(kb.at[h, pl.ds(0, HALO)], halo_r.at[h, 0])
            await_bytes(vb.at[h, pl.ds(0, HALO)], halo_r.at[h, 1])

        loop(0, BACK, lambda i: stretch(h, i))

        @pl.when(jnp.logical_not(first))
        def _():
            part_out[h, 0] = (acc_k[h, 0:HALO] * SCALE).astype(BF16)
            part_out[h, 1] = acc_v[h, 0:HALO].astype(BF16)
            part_copy(h).start()

        loop(0, BACK, lambda s: finish(h, s, False))

        @pl.when(jnp.logical_not(first))
        def _():
            loop(BACK, GROUP, lambda s: finish(h, s, False))

        @pl.when(h > 0)
        def _():
            late(h - 1)

    loop(0, HEADS, head)

    def ag_copy(h, n):
        return remote(agb.at[h, g], agb.at[h, g], ag_s.at[h], ag_r.at[h], group_dev(peer(n)))

    def spread(h):
        @pl.when(xhi == owner_of(h))
        def _():
            await_bytes(rsb.at[h], rs_r.at[h])
            agb[h, g] = jnp.sum(rsb[h], axis=0)
            loop(1, GROUP, lambda n: ag_copy(h, n).start())
            await_bytes(agb.at[h, 0:GROUP - 1], ag_r.at[h])
            local(agb.at[h], plb.at[h * 8 + dp], pl_r.at[h]).start()
            loop(1, 16, lambda n: remote(
                agb.at[h], plb.at[h * 8 + dp], pl_s.at[h], pl_r.at[h], plane_dev(n)).start())

    spread(0)
    spread(1)
    late(2)
    spread(2)

    def assemble(h):
        await_bytes(plb.at[pl.ds(h * 8, 8)], pl_r.at[h])
        for j in range(8):
            for p in range(GROUP):
                dw_ref[8 * j:8 * j + 8, (HEADS * p + h) * DH:(HEADS * p + h + 1) * DH] = (
                    plb[h * 8 + j, p])

    for h in range(HEADS):
        assemble(h)

    for a, ref in enumerate((out_ref, dq_ref, dk_ref, dv_ref)):
        await_bytes(ref, fin_r.at[a])

    def wait_main(c):
        @pl.when(jnp.logical_not(is_self(c, self_main)))
        def _():
            main_copy(c).wait_send()

    def wait_carry(c):
        @pl.when(jnp.logical_not(is_self(c, self_carry)))
        def _():
            carry_copy(c).wait_send()

    loop(0, 8, wait_main)

    @pl.when(last_slab)
    def _():
        loop(0, 8, wait_carry)

    await_bytes(vbuf.at[0:GROUP - 1], val_s.at[0])
    await_bytes(lbuf.at[0:GROUP - 1], lat_s.at[0])

    @pl.when(first)
    def _():
        await_bytes(vbuf.at[0:BACK], val_s.at[1])

    def drain(h):
        for a in range(4):
            await_bytes(qb.at[h, pl.ds(0, OWN - ROWS)], in_s.at[h, a])
            await_bytes(stg.at[a, h, pl.ds(0, OWN - ROWS)], fin_s.at[h, a])

        @pl.when(first)
        def _():
            await_bytes(kb.at[h, pl.ds(0, HALO)], halo_s.at[h, 0])
            await_bytes(vb.at[h, pl.ds(0, HALO)], halo_s.at[h, 1])

        @pl.when(jnp.logical_not(first))
        def _():
            await_bytes(part_out.at[h], part_s.at[h])

        def wait_rs(j):
            @pl.when(jnp.logical_not(rs_self(h, j)))
            def _():
                rs_copy(h, j).wait_send()

        loop(0, 8, wait_rs)

        @pl.when(xhi == owner_of(h))
        def _():
            await_bytes(agb.at[h, 0:GROUP - 1], ag_s.at[h])
            await_bytes(plb.at[0:15], pl_s.at[h])

    loop(0, HEADS, drain)


def on_device(enc_feat, conv_w, w_lat, q_raw, k_raw, v_in, valid, d_out):
    feat = enc_feat.reshape(ROWS, enc_feat.shape[3])
    wcat = jnp.concatenate([conv_w[0], conv_w[1], conv_w[1], conv_w[2]], axis=1)
    valid_tile = jnp.broadcast_to(valid, (8, 128))
    result = jax.ShapeDtypeStruct((ROWS, q_raw.shape[2]), BF16)
    anywhere = pl.BlockSpec(memory_space=pl.ANY)
    vmem = pl.BlockSpec(memory_space=pltpu.VMEM)
    dma = pltpu.SemaphoreType.DMA
    out, dq, dk, dv, dw = pl.pallas_call(
        kernel,
        out_shape=(result, result, result, result,
                   jax.ShapeDtypeStruct(w_lat.shape, F32)),
        in_specs=[vmem, vmem, vmem] + [anywhere] * 5,
        out_specs=(anywhere,) * 4 + (vmem,),
        scratch_shapes=[
            pltpu.VMEM((HEADS, OWN, DH), BF16),
            pltpu.VMEM((HEADS, OWN, DH), BF16),
            pltpu.VMEM((HEADS, HALO + OWN, DH), BF16),
            pltpu.VMEM((HEADS, HALO + OWN, DH), BF16),
            pltpu.VMEM((HEADS, HALO + OWN, DH), F32),
            pltpu.VMEM((HEADS, HALO + OWN, DH), F32),
            pltpu.VMEM((4, HEADS, OWN, DH), BF16),
            pltpu.VMEM((HEADS, 2, HALO, DH), BF16),
            pltpu.VMEM((HEADS, 2, HALO, DH), BF16),
            pltpu.VMEM((HALO + OWN, ROWS), F32),
            pltpu.VMEM((BACK + GROUP, 8, 128), jnp.int32),
            pltpu.VMEM((192, HEADS * DH), BF16),
            pltpu.VMEM((GROUP, 128, 128), BF16),
            pltpu.VMEM((8, 32, 128), F32),
            pltpu.VMEM((9, 32, 128), F32),
            pltpu.VMEM((HEADS, 64, 128), F32),
            pltpu.VMEM((HEADS, 16, 8, 128), F32),
            pltpu.VMEM((HEADS, GROUP, 8, 128), F32),
            pltpu.VMEM((HEADS * 8, GROUP, 8, 128), F32),
            dma((HEADS, 4)), dma((HEADS, 4)),
            dma((HEADS, 4)), dma((4,)),
            dma((HEADS, 2)), dma((HEADS, 2)),
            dma((HEADS,)), dma((HEADS,)),
            dma((2,)), dma((2,)),
            dma((1,)), dma((1,)),
            dma((2, 8)), dma((1,)),
            dma((HEADS, 8)), dma((HEADS,)),
            dma((HEADS,)), dma((HEADS,)),
            dma((HEADS,)), dma((HEADS,)),
            dma((1,)),
        ],
        name="slab_attention",
        compiler_params=pltpu.CompilerParams(
            collective_id=0, has_side_effects=True, vmem_limit_bytes=60 * 1024 * 1024),
    )(valid_tile, feat, wcat, w_lat, q_raw[0], k_raw[0], v_in[0], d_out[0])
    return out[None], dq[None], dk[None], dv[None], dw


def solution(mesh):
    tokens = P("dp", "ctx", None)
    return jax.shard_map(
        on_device,
        mesh=mesh,
        in_specs=(P(None, ("dp", "ctx"), None, None), P(), P(), tokens, tokens, tokens,
                  P("dp", "ctx"), tokens),
        out_specs=(tokens, tokens, tokens, tokens, P()),
        check_vma=False,
    )
```

time: 839 us -> 189 us (0.23)
  waiting for transfers between devices: 539 us -> 0 us
  Pallas kernels: 0 us -> 174 us
  starting transfers between devices: 91.7 us -> 0 us
  local copies, waits for them, and re-layouts: 99 us -> 11.2 us
  matrix products: 57.4 us -> 0 us
  other arithmetic: 34 us -> 0.89 us
  between operations: 15.1 us -> 1.32 us
    ppermute x21 -> x0, waiting for transfers between devices: 372 us -> none  [from_behind(): return lax.ppermute(value, axis, pairs)]
    pallas_call x0 -> x1, Pallas kernels: none -> 174 us  [on_device(): pl.pallas_call(kernel, out_shape=(result, result, result, result, jax.Sha...]
    psum x1 -> x0, waiting for transfers between devices: 145 us -> none  [on_device(): dw_lat = lax.psum(local_grad, ('dp', 'ctx'))]
    ppermute x21 -> x0, starting transfers between devices: 84.2 us -> none  [from_behind(): return lax.ppermute(value, axis, pairs)]
    dot_general x35 -> x0, matrix products: 32.4 us -> none  [the longest x6 10.2 us: attend(): jnp.einsum('qhd,khd->hqk', grad_heads, value_heads, preferred_element_typ...]
    dynamic_slice x25 -> x0, local copies, waits for them, and re-layouts: 28.6 us -> none  [the longest x24 28.5 us: on_device(): lax.map(per_group, (split_heads(query), split_heads(window_keys), split_h...]
    convert_element_type x7 -> x0, other arithmetic: 26.9 us -> none  [the longest x6 23.1 us: attend(): probs_low = probs.astype(jnp.bfloat16)]
    unnamed x42 -> x16, local copies, waits for them, and re-layouts: 35.6 us -> 9.64 us
  transfers between devices with their start and end apart: 23 -> 0, of which waited for: 16 -> 0; matrix products, arithmetic and copies ran while one was open for 6% -> 0% of each run, Pallas kernels for 0% -> 0%
where the time goes in v1:
time: 189 us; the launch traced here: 188 us
  Pallas kernels  174 us (92%)
  local copies, waits for them, and re-layouts  11.2 us (6%)
    pallas_call x1, Pallas kernels, on_device(): pl.pallas_call(kernel, out_shape=(result, result, result, result, jax.Sha...  174 us
    unnamed x16, local copies, waits for them, and re-layouts  9.64 us

profile of v1, /device:TPU:1, one launch (start us, length us, event | category | flops | bytes accessed | tf_op | source)
XLA Modules:
  0.0 187.5 jit_solution(4540829978356872317)
XLA Ops:
  1.3 0.6 broadcast_in_dim.20.valid_ref
  1.9 0.9 fusion
  2.8 0.1 copy.16
  2.9 0.1 copy.17
  3.0 0.1 copy.18
  3.2 0.9 pad_maximum_fusion.wcat_ref
  4.1 174.2 %slab_attention.1 = (bf16[256,3072]{1,0:T(8,128)(2,1)}, bf16[256,3072]{1,0:T(8,128)(2,1)}, bf16[256,3072]{1,0:T(8,128)(2,1)}, bf16[256,3072]{1,0:T(8,128)(2,1)}, f32[64,3072]{1,0:T(8,128)}) custom-call(s32[8,128]{1,0:T(8,128)} %broadcast_in_dim.20.valid_ref, bf16[256,512]{1,0:T(8,128)(2,1)} %bitcast.25, bf16[512,256]{1,0:T(8,128)(2,1)} %pad_maximum_fusion.wcat_ref, ...), custom_call_target="tpu_custom_call" | custom-call | tf_op jit(solution)/shard_map/slab_attention/pallas_call | solution.py:471
  178.2 0.0 copy-start.2
  178.3 2.8 %copy.25 = bf16[1,256,3072]{2,1,0:T(8,128)(2,1)} copy(bf16[1,256,3072]{2,1,0:T(8,128)(2,1)} %bitcast.17) | data formatting | bytes 3145728
  181.0 0.0 copy-done.2
  181.0 0.0 copy-start.1
  181.0 1.1 copy.26
  182.2 0.8 copy-done.1
  183.0 0.0 copy-start
  183.0 1.1 copy.27
  184.1 0.8 copy-done
  185.0 0.0 copy-start.3
  185.0 1.1 copy.28
  186.1 0.5 copy-done.3
  186.7 0.9 copy.29
Async XLA Ops:
  178.2 2.8 %copy-start.2 = (bf16[256,3072]{1,0:T(8,128)(2,1)S(1)}, bf16[256,3072]{1,0:T(8,128)(2,1)}, u32[]{:S(2)}) copy-start(bf16[256,3072]{1,0:T(8,128)(2,1)} %get-tuple-element.11) | copy-start | bytes 4718596
  181.0 2.0 %copy-start.1 = (bf16[256,3072]{1,0:T(8,128)(2,1)S(1)}, bf16[256,3072]{1,0:T(8,128)(2,1)}, u32[]{:S(2)}) copy-start(bf16[256,3072]{1,0:T(8,128)(2,1)} %get-tuple-element.12) | copy-start | bytes 4718596
  183.0 2.0 %copy-start = (bf16[256,3072]{1,0:T(8,128)(2,1)S(1)}, bf16[256,3072]{1,0:T(8,128)(2,1)}, u32[]{:S(2)}) copy-start(bf16[256,3072]{1,0:T(8,128)(2,1)} %get-tuple-element.13) | copy-start | bytes 4718596
  185.0 1.7 copy-start.3

commit v2 on v1

--- a/solution.py
+++ b/solution.py
@@ -36,9 +36,9 @@
 
 
 def kernel(
-    valid_ref, feat_ref, wcat_ref, wlat_ref, q_ref, k_ref, v_ref, do_ref,
+    count_ref, feat_ref, taps_ref, wlat_ref, q_ref, k_ref, v_ref, do_ref,
     out_ref, dq_ref, dk_ref, dv_ref, dw_ref,
-    qb, dob, kb, vb, acc_k, acc_v, stg, part_out, part_in, bias, vbuf, w2, lbuf,
+    qb, dob, kb, vb, acc_k, acc_v, stg, part_out, part_in, bias, vbuf, valid_ref, w2, lbuf,
     pk_out, pk_in, dwp, rsb, agb, plb,
     in_s, in_r, fin_s, fin_r, halo_s, halo_r, part_s, part_r, val_s, val_r,
     lat_s, lat_r, enc_s, enc_r, rs_s, rs_r, ag_s, ag_r, pl_s, pl_r, loc,
@@ -113,8 +113,9 @@
 
     local(wlat_ref.at[:, pl.ds(pl.multiple_of(g * HEADS * DH, DH), HEADS * DH)],
           w2.at[pl.ds(64, 64)], loc.at[0]).start()
-    a4 = dot(feat_ref[...], wcat_ref[:, 0:128]).reshape(8, 2, 16, 128)
-    b4 = dot(feat_ref[...], wcat_ref[:, 128:256]).reshape(8, 2, 16, 128)
+    valid_ref[...] = jnp.full((8, 128), count_ref[0, 0], jnp.int32)
+    a4 = last_last(feat_ref[...], taps_ref[0:128]).reshape(8, 2, 16, 128)
+    b4 = last_last(feat_ref[...], taps_ref[64:192]).reshape(8, 2, 16, 128)
     mix = a4[:, 1] + b4[:, 0]
     low = lax.broadcasted_iota(jnp.int32, (8, 16, 128), 2) < 64
     pk_out[:, 0:16, :] = jnp.where(low, a4[:, 0], mix)
@@ -268,6 +269,10 @@
         send_result(h, 0, i)
         send_result(h, 1, i)
 
+    def send_sums(h, s):
+        send_result(h, 2, s)
+        send_result(h, 3, s)
+
     def finish(h, s, with_part):
         rows = pl.ds(pl.multiple_of(HALO + s * ROWS, ROWS), ROWS)
         dk = acc_k[h, rows] * SCALE
@@ -279,8 +284,10 @@
         own = pl.ds(pl.multiple_of(s * ROWS, ROWS), ROWS)
         stg[2, h, own] = dk.astype(BF16)
         stg[3, h, own] = dv.astype(BF16)
-        send_result(h, 2, s)
-        send_result(h, 3, s)
+
+        @pl.when(h < HEADS - 1)
+        def _():
+            send_sums(h, s)
 
     def owner_of(h):
         return h % 2
@@ -379,21 +386,27 @@
     def ag_copy(h, n):
         return remote(agb.at[h, g], agb.at[h, g], ag_s.at[h], ag_r.at[h], group_dev(peer(n)))
 
-    def spread(h):
+    def add_up(h):
         @pl.when(xhi == owner_of(h))
         def _():
             await_bytes(rsb.at[h], rs_r.at[h])
             agb[h, g] = jnp.sum(rsb[h], axis=0)
             loop(1, GROUP, lambda n: ag_copy(h, n).start())
+
+    def spread(h):
+        @pl.when(xhi == owner_of(h))
+        def _():
             await_bytes(agb.at[h, 0:GROUP - 1], ag_r.at[h])
             local(agb.at[h], plb.at[h * 8 + dp], pl_r.at[h]).start()
             loop(1, 16, lambda n: remote(
                 agb.at[h], plb.at[h * 8 + dp], pl_s.at[h], pl_r.at[h], plane_dev(n)).start())
 
-    spread(0)
-    spread(1)
+    add_up(0)
     late(2)
-    spread(2)
+    add_up(1)
+    add_up(2)
+    loop(0, GROUP, lambda s: send_sums(HEADS - 1, s))
+    loop(0, HEADS, spread)
 
     def assemble(h):
         await_bytes(plb.at[pl.ds(h * 8, 8)], pl_r.at[h])
@@ -460,19 +473,38 @@
     loop(0, HEADS, drain)
 
 
+def settle(*refs):
+    srcs, dsts, bufs, (sems_in, sems_out) = refs[0:5], refs[5:10], refs[10:15], refs[15:17]
+    pieces = []
+    for src, dst, buf in zip(srcs, dsts, bufs):
+        half = src.shape[0] // 2
+        for at in (0, half):
+            cut = pl.ds(at, half)
+            n = len(pieces)
+            pieces.append((
+                pltpu.make_async_copy(src.at[cut], buf.at[cut], sems_in.at[n]),
+                pltpu.make_async_copy(buf.at[cut], dst.at[cut], sems_out.at[n])))
+    for into, _ in pieces:
+        into.start()
+    for into, outof in pieces:
+        into.wait()
+        outof.start()
+    for _, outof in pieces:
+        outof.wait()
+
+
 def on_device(enc_feat, conv_w, w_lat, q_raw, k_raw, v_in, valid, d_out):
     feat = enc_feat.reshape(ROWS, enc_feat.shape[3])
-    wcat = jnp.concatenate([conv_w[0], conv_w[1], conv_w[1], conv_w[2]], axis=1)
-    valid_tile = jnp.broadcast_to(valid, (8, 128))
+    taps = conv_w.swapaxes(1, 2).reshape(-1, conv_w.shape[1])
     result = jax.ShapeDtypeStruct((ROWS, q_raw.shape[2]), BF16)
     anywhere = pl.BlockSpec(memory_space=pl.ANY)
     vmem = pl.BlockSpec(memory_space=pltpu.VMEM)
     dma = pltpu.SemaphoreType.DMA
-    out, dq, dk, dv, dw = pl.pallas_call(
+    results = pl.pallas_call(
         kernel,
         out_shape=(result, result, result, result,
                    jax.ShapeDtypeStruct(w_lat.shape, F32)),
-        in_specs=[vmem, vmem, vmem] + [anywhere] * 5,
+        in_specs=[pl.BlockSpec(memory_space=pltpu.SMEM), vmem, vmem] + [anywhere] * 5,
         out_specs=(anywhere,) * 4 + (vmem,),
         scratch_shapes=[
             pltpu.VMEM((HEADS, OWN, DH), BF16),
@@ -486,6 +518,7 @@
             pltpu.VMEM((HEADS, 2, HALO, DH), BF16),
             pltpu.VMEM((HALO + OWN, ROWS), F32),
             pltpu.VMEM((BACK + GROUP, 8, 128), jnp.int32),
+            pltpu.VMEM((8, 128), jnp.int32),
             pltpu.VMEM((192, HEADS * DH), BF16),
             pltpu.VMEM((GROUP, 128, 128), BF16),
             pltpu.VMEM((8, 32, 128), F32),
@@ -509,7 +542,16 @@
         name="slab_attention",
         compiler_params=pltpu.CompilerParams(
             collective_id=0, has_side_effects=True, vmem_limit_bytes=60 * 1024 * 1024),
-    )(valid_tile, feat, wcat, w_lat, q_raw[0], k_raw[0], v_in[0], d_out[0])
+    )(valid, feat, taps, w_lat, q_raw[0], k_raw[0], v_in[0], d_out[0])
+    out, dq, dk, dv, dw = pl.pallas_call(
+        settle,
+        out_shape=tuple(jax.ShapeDtypeStruct(r.shape, r.dtype) for r in results),
+        in_specs=[anywhere] * 5,
+        out_specs=(anywhere,) * 5,
+        scratch_shapes=[pltpu.VMEM(r.shape, r.dtype) for r in results] + [dma((10,)), dma((10,))],
+        name="settle",
+        compiler_params=pltpu.CompilerParams(vmem_limit_bytes=60 * 1024 * 1024),
+    )(*results)
     return out[None], dq[None], dk[None], dv[None], dw
 
 

time: 189 us -> 170 us (0.90)
  local copies, waits for them, and re-layouts: 11.2 us -> 0 us
  Pallas kernels: 174 us -> 166 us
    pallas_call x1, Pallas kernels: 174 us -> 160 us  [on_device(): pl.pallas_call(kernel, out_shape=(result, result, result, result, jax.Sha...]
    unnamed x16 -> x0, local copies, waits for them, and re-layouts: 9.64 us -> none
    pallas_call x0 -> x1, Pallas kernels: none -> 5.77 us  [on_device(): pl.pallas_call(settle, out_shape=tuple((jax.ShapeDtypeStruct(r.shape, r.d...]
where the time goes in v2:
time: 170 us; the launch traced here: 167 us
  Pallas kernels  166 us (98%)
    pallas_call x1, Pallas kernels, on_device(): pl.pallas_call(kernel, out_shape=(result, result, result, result, jax.Sha...  160 us
    pallas_call x1, Pallas kernels, on_device(): pl.pallas_call(settle, out_shape=tuple((jax.ShapeDtypeStruct(r.shape, r.d...  5.77 us

profile of v2, /device:TPU:1, one launch (start us, length us, event | category | flops | bytes accessed | tf_op | source)
XLA Modules:
  0.0 167.4 jit_solution(15247228304763561782)
XLA Ops:
  1.3 160.3 %slab_attention.1 = (bf16[256,3072]{1,0:T(8,128)(2,1)}, bf16[256,3072]{1,0:T(8,128)(2,1)}, bf16[256,3072]{1,0:T(8,128)(2,1)}, bf16[256,3072]{1,0:T(8,128)(2,1)}, f32[64,3072]{1,0:T(8,128)}) custom-call(s32[1,1]{1,0:T(1,128)S(6)} %copy.13.count_ref, bf16[256,512]{1,0:T(8,128)(2,1)} %bitcast.16, bf16[192,512]{1,0:T(8,128)(2,1)} %bitcast.17, ...), custom_call_target="tpu_custom_call" | custom-call | tf_op jit(solution)/shard_map/slab_attention/pallas_call | solution.py:503
  161.6 5.8 %settle.1 = (bf16[256,3072]{1,0:T(8,128)(2,1)}, bf16[256,3072]{1,0:T(8,128)(2,1)}, bf16[256,3072]{1,0:T(8,128)(2,1)}, bf16[256,3072]{1,0:T(8,128)(2,1)}, f32[64,3072]{1,0:T(8,128)}) custom-call(bf16[256,3072]{1,0:T(8,128)(2,1)} %get-tuple-element.15.refs_0_, bf16[256,3072]{1,0:T(8,128)(2,1)} %get-tuple-element.16.refs_1_, ...), custom_call_target="tpu_custom_call" | custom-call | tf_op jit(solution)/shard_map/settle/pallas_call | solution.py:546

commit v3 on v1

--- a/solution.py
+++ b/solution.py
@@ -36,9 +36,9 @@
 
 
 def kernel(
-    valid_ref, feat_ref, wcat_ref, wlat_ref, q_ref, k_ref, v_ref, do_ref,
+    count_ref, feat_ref, taps_ref, wlat_ref, q_ref, k_ref, v_ref, do_ref,
     out_ref, dq_ref, dk_ref, dv_ref, dw_ref,
-    qb, dob, kb, vb, acc_k, acc_v, stg, part_out, part_in, bias, vbuf, w2, lbuf,
+    qb, dob, kb, vb, acc_k, acc_v, stg, part_out, part_in, bias, vbuf, valid_ref, w2, lbuf,
     pk_out, pk_in, dwp, rsb, agb, plb,
     in_s, in_r, fin_s, fin_r, halo_s, halo_r, part_s, part_r, val_s, val_r,
     lat_s, lat_r, enc_s, enc_r, rs_s, rs_r, ag_s, ag_r, pl_s, pl_r, loc,
@@ -113,8 +113,9 @@
 
     local(wlat_ref.at[:, pl.ds(pl.multiple_of(g * HEADS * DH, DH), HEADS * DH)],
           w2.at[pl.ds(64, 64)], loc.at[0]).start()
-    a4 = dot(feat_ref[...], wcat_ref[:, 0:128]).reshape(8, 2, 16, 128)
-    b4 = dot(feat_ref[...], wcat_ref[:, 128:256]).reshape(8, 2, 16, 128)
+    valid_ref[...] = jnp.full((8, 128), count_ref[0, 0], jnp.int32)
+    a4 = last_last(feat_ref[...], taps_ref[0:128]).reshape(8, 2, 16, 128)
+    b4 = last_last(feat_ref[...], taps_ref[64:192]).reshape(8, 2, 16, 128)
     mix = a4[:, 1] + b4[:, 0]
     low = lax.broadcasted_iota(jnp.int32, (8, 16, 128), 2) < 64
     pk_out[:, 0:16, :] = jnp.where(low, a4[:, 0], mix)
@@ -186,15 +187,16 @@
         kb[:, 0:HALO, :] = jnp.zeros((HEADS, HALO, DH), BF16)
         vb[:, 0:HALO, :] = jnp.zeros((HEADS, HALO, DH), BF16)
         vbuf[0:BACK] = jnp.zeros((BACK, 8, 128), jnp.int32)
+        lbuf[0:BACK] = jnp.zeros((BACK, 128, 128), BF16)
 
     await_bytes(pk_in, enc_r.at[0])
     before = jnp.concatenate(
         [jnp.where(ctx == 0, jnp.zeros((1, 32, 128), F32), pk_in[0:1]), pk_in[1:8]], axis=0)
     x = (pk_in[1:9] + pltpu.roll(before, 64, 2)).reshape(ROWS, 128)
     lat_low = lax.broadcasted_iota(jnp.int32, (128, 128), 1) < 64
-    lbuf[g] = jnp.where(lat_low, x[0:128], pltpu.roll(x[128:256], 64, 1)).astype(BF16)
+    lbuf[BACK + g] = jnp.where(lat_low, x[0:128], pltpu.roll(x[128:256], 64, 1)).astype(BF16)
     loop(1, GROUP, lambda n: remote(
-        lbuf.at[g], lbuf.at[g], lat_s.at[0], lat_r.at[0], group_dev(peer(n))).start())
+        lbuf.at[BACK + g], lbuf.at[BACK + g], lat_s.at[0], lat_r.at[0], group_dev(peer(n))).start())
 
     send_head(1)
     send_head(2)
@@ -222,6 +224,16 @@
     loop(0, BACK + GROUP, make_bias)
     local(wlat_ref.at[:, pl.ds(0, HEADS * DH)], w2.at[pl.ds(64, 64)], loc.at[0]).wait()
     await_bytes(lbuf.at[0:GROUP - 1], lat_r.at[0])
+    halo_latents = remote(lbuf.at[pl.ds(GROUP, BACK)], lbuf.at[pl.ds(0, BACK)],
+                          lat_s.at[1], lat_r.at[1], partner)
+
+    @pl.when(first)
+    def _():
+        halo_latents.start()
+
+    @pl.when(jnp.logical_not(first))
+    def _():
+        await_bytes(lbuf.at[0:BACK], lat_r.at[1])
 
     def halo_copy(h, a):
         buf = (kb, vb)[a]
@@ -279,36 +291,48 @@
         own = pl.ds(pl.multiple_of(s * ROWS, ROWS), ROWS)
         stg[2, h, own] = dk.astype(BF16)
         stg[3, h, own] = dv.astype(BF16)
+
         send_result(h, 2, s)
         send_result(h, 3, s)
 
-    def owner_of(h):
-        return h % 2
+    def owner_of(h, j):
+        return (h + j) % 2
+
+    def owns(h):
+        return xhi == owner_of(h, dp)
 
     def rs_copy(h, j):
         return remote(
             dwp.at[h, pl.ds(pl.multiple_of(8 * j, 8), 8)], rsb.at[h, dp * 2 + xhi],
-            rs_s.at[h, j], rs_r.at[h], (j, owner_of(h) * GROUP + g))
+            rs_s.at[h, j], rs_r.at[h], (j, owner_of(h, j) * GROUP + g))
 
     def rs_self(h, j):
-        return jnp.logical_and(j == dp, xhi == owner_of(h))
-
-    def late(h):
+        return jnp.logical_and(j == dp, owns(h))
+
+    def own_sums(h):
+        loop(0, BACK, lambda s: finish(h, s, False))
+
+        @pl.when(jnp.logical_not(first))
+        def _():
+            loop(BACK, GROUP, lambda s: finish(h, s, False))
+
+    def late_sums(h):
         @pl.when(first)
         def _():
             await_bytes(part_in.at[h], part_r.at[h])
             loop(BACK, GROUP, lambda s: finish(h, s, True))
 
+    def share(h):
         def add(s, carry):
             top, bottom = carry
             at = pl.multiple_of(s * ROWS, ROWS)
             lat = lbuf[s]
-            top = top + first_first(lat, stg[3, h, pl.ds(at, 128)])
-            bottom = bottom + first_first(lat, stg[3, h, pl.ds(at + 128, 128)])
+            top = top + first_first(lat, acc_v[h, pl.ds(at, 128)].astype(BF16))
+            bottom = bottom + first_first(lat, acc_v[h, pl.ds(at + 128, 128)].astype(BF16))
             return top, bottom
 
         zeros = jnp.zeros((128, 128), F32)
-        top, bottom = lax.fori_loop(0, GROUP, add, (zeros, zeros))
+        top, bottom = lax.fori_loop(0, BACK + GROUP, add, (zeros, zeros))
         dwp[h] = top[0:64] + bottom[64:128]
 
         def send(j):
@@ -323,12 +347,34 @@
 
         loop(0, 8, send)
 
+    def ag_copy(h, n):
+        return remote(agb.at[h, g], agb.at[h, g], ag_s.at[h], ag_r.at[h], group_dev(peer(n)))
+
+    def add_up(h):
+        @pl.when(owns(h))
+        def _():
+            await_bytes(rsb.at[h], rs_r.at[h])
+            agb[h, g] = jnp.sum(rsb[h], axis=0)
+            loop(1, GROUP, lambda n: ag_copy(h, n).start())
+
+    def spread(h):
+        @pl.when(owns(h))
+        def _():
+            await_bytes(agb.at[h, 0:GROUP - 1], ag_r.at[h])
+            local(agb.at[h], plb.at[h * 8 + dp], pl_r.at[h]).start()
+            loop(1, 16, lambda n: remote(
+                agb.at[h], plb.at[h * 8 + dp], pl_s.at[h], pl_r.at[h], plane_dev(n)).start())
+
     def head(h):
+        @pl.when(h == 2)
+        def _():
+            add_up(0)
+
         for a, (_, buf, off) in enumerate(arrays):
             await_bytes(buf.at[h, pl.ds(off, OWN)], in_r.at[h, a])
 
         def add_latents(s):
-            lat = lbuf[s]
+            lat = lbuf[BACK + s]
             at = pl.multiple_of(HALO + s * ROWS, ROWS)
             cols = pl.ds(pl.multiple_of(h * DH, DH), DH)
             upper = pl.ds(at, 128)
@@ -364,36 +410,27 @@
             part_out[h, 1] = acc_v[h, 0:HALO].astype(BF16)
             part_copy(h).start()
 
-        loop(0, BACK, lambda s: finish(h, s, False))
-
-        @pl.when(jnp.logical_not(first))
-        def _():
-            loop(BACK, GROUP, lambda s: finish(h, s, False))
-
-        @pl.when(h > 0)
-        def _():
-            late(h - 1)
+        share(h)
+
+        @pl.when(h == 0)
+        def _():
+            own_sums(0)
+
+        @pl.when(h == 1)
+        def _():
+            late_sums(0)
 
     loop(0, HEADS, head)
 
-    def ag_copy(h, n):
-        return remote(agb.at[h, g], agb.at[h, g], ag_s.at[h], ag_r.at[h], group_dev(peer(n)))
-
-    def spread(h):
-        @pl.when(xhi == owner_of(h))
-        def _():
-            await_bytes(rsb.at[h], rs_r.at[h])
-            agb[h, g] = jnp.sum(rsb[h], axis=0)
-            loop(1, GROUP, lambda n: ag_copy(h, n).start())
-            await_bytes(agb.at[h, 0:GROUP - 1], ag_r.at[h])
-            local(agb.at[h], plb.at[h * 8 + dp], pl_r.at[h]).start()
-            loop(1, 16, lambda n: remote(
-                agb.at[h], plb.at[h * 8 + dp], pl_s.at[h], pl_r.at[h], plane_dev(n)).start())
-
+    add_up(1)
     spread(0)
+    add_up(2)
+    own_sums(1)
+    late_sums(1)
+    own_sums(2)
     spread(1)
-    late(2)
     spread(2)
+    late_sums(2)
 
     def assemble(h):
         await_bytes(plb.at[pl.ds(h * 8, 8)], pl_r.at[h])
@@ -430,6 +467,7 @@
     @pl.when(first)
     def _():
         await_bytes(vbuf.at[0:BACK], val_s.at[1])
+        await_bytes(lbuf.at[0:BACK], lat_s.at[1])
 
     def drain(h):
         for a in range(4):
@@ -452,7 +490,7 @@
 
         loop(0, 8, wait_rs)
 
-        @pl.when(xhi == owner_of(h))
+        @pl.when(owns(h))
         def _():
             await_bytes(agb.at[h, 0:GROUP - 1], ag_s.at[h])
             await_bytes(plb.at[0:15], pl_s.at[h])
@@ -460,20 +498,29 @@
     loop(0, HEADS, drain)
 
 
+def settle(*refs):
+    srcs, dsts, sem = refs[0:5], refs[5:10], refs[10]
+    copies = [pltpu.make_async_copy(src, dst, sem.at[n])
+              for n, (src, dst) in enumerate(zip(srcs, dsts))]
+    for copy in copies:
+        copy.start()
+    for copy in copies:
+        copy.wait()
+
+
 def on_device(enc_feat, conv_w, w_lat, q_raw, k_raw, v_in, valid, d_out):
     feat = enc_feat.reshape(ROWS, enc_feat.shape[3])
-    wcat = jnp.concatenate([conv_w[0], conv_w[1], conv_w[1], conv_w[2]], axis=1)
-    valid_tile = jnp.broadcast_to(valid, (8, 128))
-    result = jax.ShapeDtypeStruct((ROWS, q_raw.shape[2]), BF16)
+    taps = conv_w.swapaxes(1, 2).reshape(-1, conv_w.shape[1])
+    result = pltpu.VMEM((ROWS, q_raw.shape[2]), BF16)
     anywhere = pl.BlockSpec(memory_space=pl.ANY)
     vmem = pl.BlockSpec(memory_space=pltpu.VMEM)
     dma = pltpu.SemaphoreType.DMA
-    out, dq, dk, dv, dw = pl.pallas_call(
+    results = pl.pallas_call(
         kernel,
         out_shape=(result, result, result, result,
-                   jax.ShapeDtypeStruct(w_lat.shape, F32)),
-        in_specs=[vmem, vmem, vmem] + [anywhere] * 5,
-        out_specs=(anywhere,) * 4 + (vmem,),
+                   pltpu.VMEM(w_lat.shape, F32)),
+        in_specs=[pl.BlockSpec(memory_space=pltpu.SMEM), vmem, vmem] + [anywhere] * 5,
+        out_specs=(vmem,) * 5,
         scratch_shapes=[
             pltpu.VMEM((HEADS, OWN, DH), BF16),
             pltpu.VMEM((HEADS, OWN, DH), BF16),
@@ -486,8 +533,9 @@
             pltpu.VMEM((HEADS, 2, HALO, DH), BF16),
             pltpu.VMEM((HALO + OWN, ROWS), F32),
             pltpu.VMEM((BACK + GROUP, 8, 128), jnp.int32),
+            pltpu.VMEM((8, 128), jnp.int32),
             pltpu.VMEM((192, HEADS * DH), BF16),
-            pltpu.VMEM((GROUP, 128, 128), BF16),
+            pltpu.VMEM((BACK + GROUP, 128, 128), BF16),
             pltpu.VMEM((8, 32, 128), F32),
             pltpu.VMEM((9, 32, 128), F32),
             pltpu.VMEM((HEADS, 64, 128), F32),
@@ -499,7 +547,7 @@
             dma((HEADS, 2)), dma((HEADS, 2)),
             dma((HEADS,)), dma((HEADS,)),
             dma((2,)), dma((2,)),
-            dma((1,)), dma((1,)),
+            dma((2,)), dma((2,)),
             dma((2, 8)), dma((1,)),
             dma((HEADS, 8)), dma((HEADS,)),
             dma((HEADS,)), dma((HEADS,)),
@@ -508,8 +556,17 @@
         ],
         name="slab_attention",
         compiler_params=pltpu.CompilerParams(
-            collective_id=0, has_side_effects=True, vmem_limit_bytes=60 * 1024 * 1024),
-    )(valid_tile, feat, wcat, w_lat, q_raw[0], k_raw[0], v_in[0], d_out[0])
+            collective_id=0, has_side_effects=True, vmem_limit_bytes=57 * 1024 * 1024),
+    )(valid, feat, taps, w_lat, q_raw[0], k_raw[0], v_in[0], d_out[0])
+    out, dq, dk, dv, dw = pl.pallas_call(
+        settle,
+        out_shape=tuple(jax.ShapeDtypeStruct(r.shape, r.dtype) for r in results),
+        in_specs=[vmem] * 5,
+        out_specs=(anywhere,) * 5,
+        scratch_shapes=[dma((5,))],
+        name="settle",
+        compiler_params=pltpu.CompilerParams(vmem_limit_bytes=16 * 1024 * 1024),
+    )(*(pltpu.with_memory_space_constraint(r, pltpu.VMEM) for r in results))
     return out[None], dq[None], dk[None], dv[None], dw
 
 

time: 189 us -> 158 us (0.84)
  Pallas kernels: 174 us -> 157 us
  local copies, waits for them, and re-layouts: 11.2 us -> 0 us
    pallas_call x1 -> x2, Pallas kernels: 174 us -> 157 us  [the longest x1 154 us: on_device(): pl.pallas_call(kernel, out_shape=(result, result, result, result, pltpu.V...]
    unnamed x16 -> x0, local copies, waits for them, and re-layouts: 9.64 us -> none
where the time goes in v3:
time: 158 us
  Pallas kernels  157 us (99%)
    pallas_call x1, Pallas kernels, on_device(): pl.pallas_call(kernel, out_shape=(result, result, result, result, pltpu.V...  154 us

profile of v3, /device:TPU:1, one launch (start us, length us, event | category | flops | bytes accessed | tf_op | source)
XLA Modules:
  0.0 158.1 jit_solution(18097963168825929117)
XLA Ops:
  1.3 153.8 %slab_attention.1 = (bf16[256,3072]{1,0:T(8,128)(2,1)S(1)}, bf16[256,3072]{1,0:T(8,128)(2,1)S(1)}, bf16[256,3072]{1,0:T(8,128)(2,1)S(1)}, bf16[256,3072]{1,0:T(8,128)(2,1)S(1)}, f32[64,3072]{1,0:T(8,128)S(1)}) custom-call(s32[1,1]{1,0:T(1,128)S(6)} %copy.13.count_ref, bf16[256,512]{1,0:T(8,128)(2,1)} %bitcast.16, bf16[192,512]{1,0:T(8,128)(2,1)} %bitcast.17, ...), custom_call_target="tpu_custom_call" | custom-call | tf_op jit(solution)/shard_map/slab_attention/pallas_call | solution.py:518
  155.1 3.0 %settle.1 = (bf16[256,3072]{1,0:T(8,128)(2,1)}, bf16[256,3072]{1,0:T(8,128)(2,1)}, bf16[256,3072]{1,0:T(8,128)(2,1)}, bf16[256,3072]{1,0:T(8,128)(2,1)}, f32[64,3072]{1,0:T(8,128)}) custom-call(bf16[256,3072]{1,0:T(8,128)(2,1)S(1)} %get-tuple-element.15.refs_0_, bf16[256,3072]{1,0:T(8,128)(2,1)S(1)} %get-tuple-element.16.refs_1_, ...), custom_call_target="tpu_custom_call" | custom-call | tf_op jit(solution)/shard_map/settle/pallas_call | solution.py:561

commit v4 on v3

--- a/solution.py
+++ b/solution.py
@@ -113,7 +113,7 @@
 
     local(wlat_ref.at[:, pl.ds(pl.multiple_of(g * HEADS * DH, DH), HEADS * DH)],
           w2.at[pl.ds(64, 64)], loc.at[0]).start()
-    valid_ref[...] = jnp.full((8, 128), count_ref[0, 0], jnp.int32)
+    valid_ref[...] = jnp.broadcast_to(count_ref[...], (8, 128))
     a4 = last_last(feat_ref[...], taps_ref[0:128]).reshape(8, 2, 16, 128)
     b4 = last_last(feat_ref[...], taps_ref[64:192]).reshape(8, 2, 16, 128)
     mix = a4[:, 1] + b4[:, 0]
@@ -173,9 +173,9 @@
                 return src.at[:, pl.ds(pl.multiple_of((HEADS * p + h) * DH, DH), DH)]
 
             local(cols(g), dst, in_r.at[h, a]).start()
-            loop(1, GROUP, lambda n: remote(
-                cols(peer(n)), dst, in_s.at[h, a], in_r.at[h, a],
-                group_dev(peer(n))).start())
+            loop(0, GROUP - 1, lambda n: remote(
+                cols(peer(1 + (4 * n + 1) % 7)), dst, in_s.at[h, a], in_r.at[h, a],
+                group_dev(peer(1 + (4 * n + 1) % 7))).start())
 
     send_head(0)
 
@@ -195,8 +195,14 @@
     x = (pk_in[1:9] + pltpu.roll(before, 64, 2)).reshape(ROWS, 128)
     lat_low = lax.broadcasted_iota(jnp.int32, (128, 128), 1) < 64
     lbuf[BACK + g] = jnp.where(lat_low, x[0:128], pltpu.roll(x[128:256], 64, 1)).astype(BF16)
-    loop(1, GROUP, lambda n: remote(
-        lbuf.at[BACK + g], lbuf.at[BACK + g], lat_s.at[0], lat_r.at[0], group_dev(peer(n))).start())
+    beside = g + 1 - 2 * (g % 2)
+
+    def pass_latents(p, to, n):
+        remote(lbuf.at[BACK + p], lbuf.at[BACK + p], lat_s.at[n], lat_r.at[n],
+               group_dev(to)).start()
+
+    loop(1, 4, lambda n: pass_latents(g, peer(2 * n), 0))
+    pass_latents(g, beside, 2)
 
     send_head(1)
     send_head(2)
@@ -223,7 +229,9 @@
 
     loop(0, BACK + GROUP, make_bias)
     local(wlat_ref.at[:, pl.ds(0, HEADS * DH)], w2.at[pl.ds(64, 64)], loc.at[0]).wait()
-    await_bytes(lbuf.at[0:GROUP - 1], lat_r.at[0])
+    await_bytes(lbuf.at[0:3], lat_r.at[0])
+    loop(1, 4, lambda n: pass_latents(peer(2 * n), beside, 2))
+    await_bytes(lbuf.at[0:4], lat_r.at[2])
     halo_latents = remote(lbuf.at[pl.ds(GROUP, BACK)], lbuf.at[pl.ds(0, BACK)],
                           lat_s.at[1], lat_r.at[1], partner)
 
@@ -462,7 +470,8 @@
         loop(0, 8, wait_carry)
 
     await_bytes(vbuf.at[0:GROUP - 1], val_s.at[0])
-    await_bytes(lbuf.at[0:GROUP - 1], lat_s.at[0])
+    await_bytes(lbuf.at[0:3], lat_s.at[0])
+    await_bytes(lbuf.at[0:4], lat_s.at[2])
 
     @pl.when(first)
     def _():
@@ -519,7 +528,7 @@
         kernel,
         out_shape=(result, result, result, result,
                    pltpu.VMEM(w_lat.shape, F32)),
-        in_specs=[pl.BlockSpec(memory_space=pltpu.SMEM), vmem, vmem] + [anywhere] * 5,
+        in_specs=[vmem, vmem, vmem] + [anywhere] * 5,
         out_specs=(vmem,) * 5,
         scratch_shapes=[
             pltpu.VMEM((HEADS, OWN, DH), BF16),
@@ -547,7 +556,7 @@
             dma((HEADS, 2)), dma((HEADS, 2)),
             dma((HEADS,)), dma((HEADS,)),
             dma((2,)), dma((2,)),
-            dma((2,)), dma((2,)),
+            dma((3,)), dma((3,)),
             dma((2, 8)), dma((1,)),
             dma((HEADS, 8)), dma((HEADS,)),
             dma((HEADS,)), dma((HEADS,)),

time: 158 us -> 157 us (level)
  Pallas kernels: 157 us -> 155 us
where the time goes in v4:
time: 157 us
  Pallas kernels  155 us (99%)
    pallas_call x1, Pallas kernels, on_device(): pl.pallas_call(kernel, out_shape=(result, result, result, result, pltpu.V...  152 us

profile of v4, /device:TPU:1, one launch (start us, length us, event | category | flops | bytes accessed | tf_op | source)
XLA Modules:
  0.0 156.7 jit_solution(9597202755736984688)
XLA Ops:
  1.3 152.4 %slab_attention.1 = (bf16[256,3072]{1,0:T(8,128)(2,1)S(1)}, bf16[256,3072]{1,0:T(8,128)(2,1)S(1)}, bf16[256,3072]{1,0:T(8,128)(2,1)S(1)}, bf16[256,3072]{1,0:T(8,128)(2,1)S(1)}, f32[64,3072]{1,0:T(8,128)S(1)}) custom-call(s32[1,1]{1,0:T(1,128)S(6)} %copy.13.count_ref, bf16[256,512]{1,0:T(8,128)(2,1)} %bitcast.16, bf16[192,512]{1,0:T(8,128)(2,1)} %bitcast.17, ...), custom_call_target="tpu_custom_call" | custom-call | tf_op jit(solution)/shard_map/slab_attention/pallas_call | solution.py:527
  153.7 3.0 %settle.1 = (bf16[256,3072]{1,0:T(8,128)(2,1)}, bf16[256,3072]{1,0:T(8,128)(2,1)}, bf16[256,3072]{1,0:T(8,128)(2,1)}, bf16[256,3072]{1,0:T(8,128)(2,1)}, f32[64,3072]{1,0:T(8,128)}) custom-call(bf16[256,3072]{1,0:T(8,128)(2,1)S(1)} %get-tuple-element.15.refs_0_, bf16[256,3072]{1,0:T(8,128)(2,1)S(1)} %get-tuple-element.16.refs_1_, ...), custom_call_target="tpu_custom_call" | custom-call | tf_op jit(solution)/shard_map/settle/pallas_call | solution.py:570

commit v5 on v4

--- a/solution.py
+++ b/solution.py
@@ -318,17 +318,17 @@
         return jnp.logical_and(j == dp, owns(h))
 
     def own_sums(h):
-        loop(0, BACK, lambda s: finish(h, s, False))
+        loop(0, BACK, lambda s: finish(h, (s + g) % BACK, False))
 
         @pl.when(jnp.logical_not(first))
         def _():
-            loop(BACK, GROUP, lambda s: finish(h, s, False))
+            loop(0, BACK, lambda s: finish(h, BACK + (s + g) % BACK, False))
 
     def late_sums(h):
         @pl.when(first)
         def _():
             await_bytes(part_in.at[h], part_r.at[h])
-            loop(BACK, GROUP, lambda s: finish(h, s, True))
+            loop(0, BACK, lambda s: finish(h, BACK + (s + g) % BACK, True))
 
     def share(h):
         def add(s, carry):
@@ -403,14 +403,14 @@
         acc_k[h] = jnp.zeros((HALO + OWN, DH), F32)
         acc_v[h] = jnp.zeros((HALO + OWN, DH), F32)
 
-        loop(BACK, GROUP, lambda i: stretch(h, i))
+        loop(0, BACK, lambda i: stretch(h, BACK + (i + g) % BACK))
 
         @pl.when(jnp.logical_not(first))
         def _():
             await_bytes(kb.at[h, pl.ds(0, HALO)], halo_r.at[h, 0])
             await_bytes(vb.at[h, pl.ds(0, HALO)], halo_r.at[h, 1])
 
-        loop(0, BACK, lambda i: stretch(h, i))
+        loop(0, BACK, lambda i: stretch(h, (i + g) % BACK))
 
         @pl.when(jnp.logical_not(first))
         def _():

time: 157 us -> 157 us (level)
  no operation moved by 1% of the time
where the time goes in v5:
time: 157 us
  Pallas kernels  155 us (99%)
    pallas_call x1, Pallas kernels, on_device(): pl.pallas_call(kernel, out_shape=(result, result, result, result, pltpu.V...  152 us

profile of v5, /device:TPU:1, one launch (start us, length us, event | category | flops | bytes accessed | tf_op | source)
XLA Modules:
  0.0 156.7 jit_solution(1090401973987841608)
XLA Ops:
  1.3 152.4 %slab_attention.1 = (bf16[256,3072]{1,0:T(8,128)(2,1)S(1)}, bf16[256,3072]{1,0:T(8,128)(2,1)S(1)}, bf16[256,3072]{1,0:T(8,128)(2,1)S(1)}, bf16[256,3072]{1,0:T(8,128)(2,1)S(1)}, f32[64,3072]{1,0:T(8,128)S(1)}) custom-call(s32[1,1]{1,0:T(1,128)S(6)} %copy.13.count_ref, bf16[256,512]{1,0:T(8,128)(2,1)} %bitcast.16, bf16[192,512]{1,0:T(8,128)(2,1)} %bitcast.17, ...), custom_call_target="tpu_custom_call" | custom-call | tf_op jit(solution)/shard_map/slab_attention/pallas_call | solution.py:527
  153.7 3.0 %settle.1 = (bf16[256,3072]{1,0:T(8,128)(2,1)}, bf16[256,3072]{1,0:T(8,128)(2,1)}, bf16[256,3072]{1,0:T(8,128)(2,1)}, bf16[256,3072]{1,0:T(8,128)(2,1)}, f32[64,3072]{1,0:T(8,128)}) custom-call(bf16[256,3072]{1,0:T(8,128)(2,1)S(1)} %get-tuple-element.15.refs_0_, bf16[256,3072]{1,0:T(8,128)(2,1)S(1)} %get-tuple-element.16.refs_1_, ...), custom_call_target="tpu_custom_call" | custom-call | tf_op jit(solution)/shard_map/settle/pallas_call | solution.py:570
